TPU v7x, 128 devices: a whole 4x4x4 slice. The times are simulated.
128 devices in a mesh: rows: 16 (over y, z_lo, core), reg: 8 (over z_hi, x).
Axes of the slice: x: 4, y: 4, z: 4 (z_hi: 2, z_lo: 2; z = z_hi * 2 + z_lo), core: 2. Of those that a mesh axis runs over, the one named last changes fastest.
Arguments:
- snapshots: bfloat16 [131072, 2048], P('rows', 'reg'), may hold values from -6 to 6
- rates: bfloat16 [131072, 2048], P('rows', 'reg'), may hold values from -6 to 6
- basis: bfloat16 [131072, 128], P('rows'), may hold values from -0.015625 to 0.015625
Outputs:
- gram: float32 [8384, 8384], P('rows', 'reg')
- rhs: float32 [8384, 128], P('rows')
All inputs are finite; a program needn't handle non-finite values.
Results may differ from a plain program's by a relative error of at most 0.0042.
Values may be sent and summed in bfloat16 or wider, within the bound.
A program may use at most 64 MiB of HBM per device.

v0:
```python
import jax
import jax.numpy as jnp
import numpy as np
from jax import lax
from jax.sharding import PartitionSpec as P


def make_features(states):
    upper_i, upper_j = np.triu_indices(states.shape[0])
    quad = jnp.take(states, upper_i, axis=0) * jnp.take(states, upper_j, axis=0)
    return jnp.concatenate([states, quad], axis=0).astype(jnp.bfloat16)


def block_adder(col_feat, total, piece):
    columns = lax.slice_in_dim(col_feat, 0, piece.shape[1], axis=1)
    return total + lax.dot_general(
        piece, columns, (((1,), (1,)), ((), ())), preferred_element_type=jnp.float32
    )


def per_device(snapshots, rates, basis):
    rank = basis.shape[1]
    width = rank + rank * (rank + 1) // 2
    local_time = snapshots.shape[1]
    total_time = local_time * lax.axis_size("reg")
    row_width = width // lax.axis_size("rows")
    col_width = width // lax.axis_size("reg")
    part_states = jnp.einsum("nr,nt->rt", basis, snapshots, preferred_element_type=jnp.float32)
    part_rates = jnp.einsum("nr,nt->rt", basis, rates, preferred_element_type=jnp.float32)
    empty = jnp.zeros((row_width, col_width), jnp.float32)
    states = lax.psum_scatter(part_states, "rows", scatter_dimension=1, tiled=True)
    moments = lax.psum(part_rates, "rows")
    local_feat = make_features(states)
    row_feat = lax.all_to_all(local_feat, "rows", split_axis=0, concat_axis=1, tiled=True)
    full_feat = lax.all_gather(local_feat, "rows", axis=1, tiled=True)
    col_feat = lax.all_to_all(full_feat, "reg", split_axis=0, concat_axis=1, tiled=True)
    gram = block_adder(col_feat, empty, lax.all_gather(row_feat, "reg", axis=1, tiled=True))
    rate_half = moments.astype(jnp.bfloat16)
    rhs_part = lax.dot_general(
        row_feat, rate_half, (((1,), (1,)), ((), ())), preferred_element_type=jnp.float32
    )
    rhs = lax.psum(rhs_part, "reg")
    return (gram / float(total_time), rhs / float(total_time))


def solution(mesh):
    return jax.shard_map(
        per_device,
        mesh=mesh,
        in_specs=(P("rows", "reg"), P("rows", "reg"), P("rows", None)),
        out_specs=(P("rows", "reg"), P("rows", None)),
        check_vma=False,
    )
```

profile of v0, /device:TPU:1, one launch (start us, length us, event | category | flops | bytes accessed | tf_op | source)
XLA Modules:
  0.0 394.4 jit_solution(7418192910360525687)
XLA Ops:
  7.2 1.5 copy-done
  8.8 4.6 %fusion.2 = f32[128,256]{0,1:T(8,128)} fusion(bf16[8192,128]{1,0:T(8,128)(2,1)S(1)} %copy-done, bf16[8192,256]{1,0:T(8,128)(2,1)} %param.7), kind=kOutput, calls=%fused_computation.9 | convolution fusion | flops 536870912 | bytes 6422528 | tf_op jit(solution)/shard_map/nr,nt->rt/dot_general | solution.py:28
  13.4 0.0 all-gather.5.cloned.1.call-start
  13.5 60.6 %reduce-scatter.2.cloned.1.call-done = f32[128,16]{0,1:T(8,128)} async-done(((f32[128,256]{0,1:T(8,128)}), f32[128,16]{0,1:T(8,128)}) %reduce-scatter.2.cloned.1.call-update) | async-done | bytes 8208 | tf_op jit(solution)/shard_map/reduce_scatter | solution.py:31
  74.1 0.8 copy.22
  74.9 16.4 %gather_fusion.1 = f32[8256,16]{1,0:T(8,128)} fusion(f32[128,16]{1,0:T(8,128)S(1)} %copy.22, s32[9216]{0:T(1024)S(1)} %pad_clamp_fusion), kind=kCustom, calls=%fused_computation.1.clone | custom fusion | bytes 1089792 | tf_op jit(solution)/shard_map/jit(_take)/gather | solution.py:10
  91.3 16.3 %gather_fusion = f32[8256,16]{1,0:T(8,128)} fusion(f32[128,16]{1,0:T(8,128)S(1)} %copy.22, s32[9216]{0:T(1024)S(1)} %pad_clamp_fusion.1), kind=kCustom, calls=%fused_computation.clone | custom fusion | bytes 1089792 | tf_op jit(solution)/shard_map/jit(_take)/gather | solution.py:10
  107.6 4.8 %mul.3 = bf16[8256,16]{1,0:T(8,128)(2,1)} multiply(f32[8256,16]{1,0:T(8,128)} %gather_fusion, f32[8256,16]{1,0:T(8,128)} %gather_fusion.1) | non-fusion elementwise | flops 132096 | bytes 1320960 | tf_op jit(solution)/shard_map/mul | solution.py:10
  112.3 2.1 copy.24
  114.4 0.7 maximum_convert_fusion
  115.2 1.4 convert_element_type.11
  116.6 0.8 copy.25
  117.4 7.5 %all-to-all-start = ((bf16[16,524,16]{1,2,0:T(8,128)(2,1)}), bf16[16,524,16]{1,2,0:T(8,128)(2,1)S(1)}, u32[]{:S(2)}, u32[]{:S(2)}) async-start(bf16[16,524,16]{1,2,0:T(8,128)(2,1)} %copy.25), calls=%async_computation.1 | async-start | bytes 655360 | tf_op jit(solution)/shard_map/all_to_all | solution.py:34
  125.0 3.0 fusion.3
  128.0 53.6 %all-reduce.4 = bf16[128,256]{1,0:T(8,128)(2,1)S(1)} all-reduce(f32[128,256]{1,0:T(8,128)S(1)} %fusion.3), channel_id=1, replica_groups=mesh['rows'=16,'reg'=8] {'rows'}, use_global_device_ids=true, to_apply=%region_1.3 | all-reduce | flops 32768 | bytes 196608 | tf_op jit(solution)/shard_map/psum | solution.py:32
  181.7 1.0 fusion.4
  182.7 6.5 %copy.26 = bf16[8384,256]{1,0:T(8,128)(2,1)} copy(bf16[8384,256]{0,1:T(8,128)(2,1)} %all-gather.5.cloned.1.call-done) | data formatting | bytes 8585216 | tf_op jit(solution)/shard_map/all_gather | solution.py:35
  189.2 6.5 %all-to-all-start.1 = ((bf16[8,1048,256]{2,1,0:T(8,128)(2,1)}), bf16[8,1048,256]{2,1,0:T(8,128)(2,1)}, u32[]{:S(2)}, u32[]{:S(2)}) async-start(bf16[8,1048,256]{2,1,0:T(8,128)(2,1)} %bitcast.17), calls=%async_computation.2 | async-start | bytes 8585216 | tf_op jit(solution)/shard_map/all_to_all | solution.py:36
  195.8 0.5 all-gather.3.cloned.1.call-update
  196.3 118.3 %all-reduce.3.cloned.1.call-done = f32[524,128]{1,0:T(8,128)} async-done(((f32[524,128]{1,0:T(8,128)}), f32[524,128]{1,0:T(8,128)}) %all-reduce.3.cloned.1.call-update) | async-done | bytes 268304 | tf_op jit(solution)/shard_map/psum | solution.py:42
  314.7 1.7 broadcast_multiply_fusion
  316.4 4.8 %copy.28 = bf16[8,131,8,256]{3,2,0,1:T(8,128)(2,1)} copy(bf16[8,131,8,256]{3,2,1,0:T(8,128)(2,1)} %bitcast.5) | data formatting | bytes 8585216 | tf_op jit(solution)/shard_map/all_to_all | solution.py:36
  321.2 58.6 %all-gather.3.cloned.1.call-done = bf16[524,2048]{0,1:T(8,128)(2,1)} async-done(((bf16[524,256]{0,1:T(8,128)(2,1)}), bf16[524,2048]{0,1:T(8,128)(2,1)}) %all-gather.3.cloned.1.call-update) | async-done | bytes 2146320 | tf_op jit(solution)/shard_map/all_gather | solution.py:37
  379.8 8.0 %convolution_multiply_fusion = f32[524,1048]{1,0:T(8,128)} fusion(bf16[524,2048]{0,1:T(8,128)(2,1)} %all-gather.3.cloned.1.call-done, bf16[1048,2048]{1,0:T(8,128)(2,1)} %bitcast.18), kind=kOutput, calls=%fused_computation.2 | convolution fusion | flops 2249875712 | bytes 8635520 | tf_op jit(solution)/shard_map/dot_general | solution.py:16
  (20 shorter events, 0.2 us)
Async XLA Ops:
  7.2 1.6 copy-start
  7.2 6.2 %copy-start.2 = (s32[8256]{0:T(1024)S(1)}, s32[8256]{0:T(1024)}, u32[]{:S(2)}) copy-start(s32[8256]{0:T(1024)} %constant.39) | copy-start | bytes 99076
  7.2 6.3 %copy-start.3 = (s32[8256]{0:T(1024)S(1)}, s32[8256]{0:T(1024)}, u32[]{:S(2)}) copy-start(s32[8256]{0:T(1024)} %constant.40) | copy-start | bytes 99076
  7.2 66.9 %reduce-scatter.2.cloned.1.call-start = ((), (), s32[]{:S(2)}) async-start(), calls=%async_computation.3 | async-start | bytes 139264 | tf_op jit(solution)/shard_map/reduce_scatter | solution.py:31
  13.4 169.3 %all-gather.5.cloned.1.call-start = ((), (), s32[]{:S(2)}) async-start(), calls=%async_computation.5 | async-start | bytes 4595712 | tf_op jit(solution)/shard_map/all_gather | solution.py:35
  107.6 6.9 %copy-start.4 = (f32[128,16]{0,1:T(8,128)S(1)}, f32[128,16]{0,1:T(8,128)}, u32[]{:S(2)}) copy-start(f32[128,16]{0,1:T(8,128)} %reduce-scatter.2.cloned.1.call-done) | copy-start | bytes 24580
  117.4 64.3 %all-to-all-start = ((bf16[16,524,16]{1,2,0:T(8,128)(2,1)}), bf16[16,524,16]{1,2,0:T(8,128)(2,1)S(1)}, u32[]{:S(2)}, u32[]{:S(2)}) async-start(bf16[16,524,16]{1,2,0:T(8,128)(2,1)} %copy.25), calls=%async_computation.1 | async-start | bytes 655360 | tf_op jit(solution)/shard_map/all_to_all | solution.py:34
  124.9 189.8 %all-reduce.3.cloned.1.call-start = ((), (), s32[]{:S(2)}) async-start(), calls=%async_computation.6 | async-start | bytes 540672 | tf_op jit(solution)/shard_map/psum | solution.py:42
  181.6 7.6 %copy-start.1 = (bf16[16,524,16]{1,2,0:T(8,128)(2,1)}, bf16[16,524,16]{1,2,0:T(8,128)(2,1)S(1)}, u32[]{:S(2)}) copy-start(bf16[16,524,16]{1,2,0:T(8,128)(2,1)S(1)} %all-to-all-done) | copy-start | bytes 804868
  189.2 127.1 %all-to-all-start.1 = ((bf16[8,1048,256]{2,1,0:T(8,128)(2,1)}), bf16[8,1048,256]{2,1,0:T(8,128)(2,1)}, u32[]{:S(2)}, u32[]{:S(2)}) async-start(bf16[8,1048,256]{2,1,0:T(8,128)(2,1)} %bitcast.17), calls=%async_computation.2 | async-start | bytes 8585216 | tf_op jit(solution)/shard_map/all_to_all | solution.py:36
  195.8 184.1 %all-gather.3.cloned.1.call-start = ((), (), s32[]{:S(2)}) async-start(), calls=%async_computation.4 | async-start | bytes 2949120 | tf_op jit(solution)/shard_map/all_gather | solution.py:37
Sparse Core Ops, SparseCore 0:
  13.5 60.5 reduce-scatter.1
  115.3 42.5 all-gather.4
  182.8 131.8 all-reduce.2
  317.4 62.3 all-gather.2
where the time goes:
time: 396 us; the launch traced here: 394 us
  waiting for transfers between devices  238 us (60%)
  blocking collectives  53.6 us (14%)
  local copies, waits for them, and re-layouts  50.7 us (13%)
  matrix products  16.6 us (4%)
  starting transfers between devices  14.2 us (4%)
  between operations  13.9 us (4%)
  other arithmetic  7.18 us (2%)
    psum x1, waiting for transfers between devices, per_device(): rhs = lax.psum(rhs_part, 'reg')  118 us
    reduce_scatter x1, waiting for transfers between devices, per_device(): lax.psum_scatter(part_states, 'rows', scatter_dimension=1, tiled=True)  60.6 us
    all_gather x1, waiting for transfers between devices, per_device(): lax.all_gather(row_feat, 'reg', axis=1, tiled=True)  58.6 us
    psum x1, blocking collectives, per_device(): moments = lax.psum(part_rates, 'rows')  53.6 us
    gather x2, local copies, waits for them, and re-layouts, make_features(): quad = jnp.take(states, upper_i, axis=0) * jnp.take(states, upper_j, axis=0)  32.7 us
    dot_general x1, matrix products, block_adder(): lax.dot_general(piece, columns, (((1,), (1,)), ((), ())), preferred_eleme...  8.04 us
  transfers between devices with their start and end apart: 6, of which 3 were waited for; matrix products, arithmetic and copies ran while one was open for 5% of the time, Pallas kernels for 0%

commit v1 on v0

v1 whole, which is shorter than its diff:
```python
import jax
import jax.numpy as jnp
from jax import lax
from jax.experimental import pallas as pl
from jax.experimental.pallas import tpu as pltpu
from jax.sharding import PartitionSpec as P

MESH = pl.DeviceIdType.MESH
F32 = jnp.float32
BF16 = jnp.bfloat16
CHUNKS = 8


def device_at(x, y, z, c):
    return ((y * 2 + lax.rem(z, 2)) * 2 + c, lax.div(z, 2) * 4 + x)


def exchange_kernel(
    snap_hbm, rates_hbm, basis_hbm, states_out, moments_out,
    snap, rates, basis, basis_t, part_s, part_m, land_s, land_m,
    load_sem, send_s, recv_s, send_m, recv_m,
    sg_send, sg_recv, mg_send, mg_recv,
):
    rows, reg = lax.axis_index("rows"), lax.axis_index("reg")
    c = lax.rem(rows, 2)
    zl = lax.rem(lax.div(rows, 2), 2)
    y = lax.div(rows, 4)
    x = lax.rem(reg, 4)
    zh = lax.div(reg, 4)
    z = zh * 2 + zl

    def turn(v, d):
        return lax.rem(v + d, 4)

    group = [(dy, dz, dc) for dy in range(4) for dz in range(2) for dc in range(2)][1:]

    def group_row(dy, dz, dc):
        return (turn(y, dy) * 2 + lax.rem(zl + dz, 2)) * 2 + lax.rem(c + dc, 2)

    barrier = pltpu.get_barrier_semaphore()
    for dy, dz, dc in group:
        pl.semaphore_signal(barrier, inc=1, device_id=(group_row(dy, dz, dc), reg), device_id_type=MESH)
    for d in (1, 2, 3):
        pl.semaphore_signal(barrier, inc=1, device_id=device_at(turn(x, d), y, z, c), device_id_type=MESH)
    for d in (2, 3 + 2 * zl):
        pl.semaphore_signal(barrier, inc=1, device_id=device_at(x, y, turn(z, d), c), device_id_type=MESH)

    depth = snap_hbm.shape[0] // CHUNKS
    loads = {}
    for k in range(CHUNKS):
        at = pl.ds(k * depth, depth)
        for i, (src, dst) in enumerate(((basis_hbm, basis), (snap_hbm, snap))):
            loads[i, k] = pltpu.make_async_copy(src.at[at, :], dst.at[at, :], load_sem.at[i, k])
            loads[i, k].start()
    for k in range(CHUNKS):
        at = pl.ds(k * depth, depth)
        loads[2, k] = pltpu.make_async_copy(rates_hbm.at[at, :], rates.at[at, :], load_sem.at[2, k])
        loads[2, k].start()

    total = jnp.zeros((128, 256), F32)
    for k in range(CHUNKS):
        at = pl.ds(k * depth, depth)
        loads[0, k].wait()
        loads[1, k].wait()
        turned = basis[at, :].T
        basis_t[:, at] = turned
        total += jnp.dot(turned, snap[at, :], preferred_element_type=F32)
    part_s[...] = total.reshape(16, 8, 256)

    pl.semaphore_wait(barrier, 20)
    out_s = []
    for n, (dy, dz, dc) in enumerate(group):
        to = group_row(dy, dz, dc)
        copy = pltpu.make_async_remote_copy(
            src_ref=part_s.at[to], dst_ref=land_s.at[n], send_sem=send_s.at[n], recv_sem=recv_s.at[n],
            device_id=(to, reg), device_id_type=MESH,
        )
        copy.start()
        out_s.append(copy)

    total = jnp.zeros((128, 256), F32)
    for k in range(CHUNKS):
        at = pl.ds(k * depth, depth)
        loads[2, k].wait()
        total += jnp.dot(basis_t[:, at], rates[at, :], preferred_element_type=F32)
    for b in range(8):
        for h in range(2):
            part_m[b * 2 + h] = total[b * 16:(b + 1) * 16, h * 128:(h + 1) * 128]
    out_m = []
    for n, (dy, dz, dc) in enumerate(group):
        to = group_row(dy, dz, dc)
        copy = pltpu.make_async_remote_copy(
            src_ref=part_m.at[to], dst_ref=land_m.at[n], send_sem=send_m.at[n], recv_sem=recv_m.at[n],
            device_id=(to, reg), device_id_type=MESH,
        )
        copy.start()
        out_m.append(copy)

    first = (1 - c) * y + c * z
    second = (1 - c) * z + c * x
    third = (1 - c) * x + c * y

    def peer(stage, d):
        step0, step1 = (1 - c) * d, c * d
        if stage == 1:
            return device_at(x, turn(y, step0), turn(z, step1), c)
        if stage == 2:
            return device_at(turn(x, step1), y, turn(z, step0), c)
        return device_at(turn(x, step0), turn(y, step1), z, c)

    own = (third * 4 + second) * 4 + first
    pending = []

    def gather(buf, send, recv):
        def push(at, device, n):
            copy = pltpu.make_async_remote_copy(
                src_ref=buf.at[c, at], dst_ref=buf.at[c, at], send_sem=send.at[n], recv_sem=recv.at[n],
                device_id=device, device_id_type=MESH,
            )
            copy.start()
            pending.append(copy)

        def arrive(at, n):
            pltpu.make_async_remote_copy(
                src_ref=buf.at[c, at], dst_ref=buf.at[c, at], send_sem=send.at[n], recv_sem=recv.at[n],
                device_id=device_at(x, y, z, 1 - c), device_id_type=MESH,
            ).wait_recv()

        def arrive_twin(at, n):
            pltpu.make_async_remote_copy(
                src_ref=buf.at[1 - c, at], dst_ref=buf.at[1 - c, at], send_sem=send.at[n], recv_sem=recv.at[n],
                device_id=device_at(x, y, z, 1 - c), device_id_type=MESH,
            ).wait_recv()

        twin = device_at(x, y, z, 1 - c)

        def quad(a3, a2):
            return pl.ds((a3 * 4 + a2) * 4, 4)

        def stage1():
            for d in (1, 2, 3):
                push(pl.ds(own, 1), peer(1, d), d - 1)

        def stage2():
            for d in (1, 2, 3):
                arrive(pl.ds((third * 4 + second) * 4 + turn(first, 4 - d), 1), d - 1)
            mine = quad(third, second)
            for d in (1, 2, 3):
                push(mine, peer(2, d), 2 + d)
            for d in (1, 2, 3):
                push(mine, peer(3, d), 6 + (d - 1) * 4)
            push(mine, twin, 18)

        def stage3():
            for e in (1, 2, 3):
                at = quad(third, turn(second, 4 - e))
                arrive(at, 2 + e)
                for d in (1, 2, 3):
                    push(at, peer(3, d), 6 + (d - 1) * 4 + e)
                push(at, twin, 18 + e)

        def stage4():
            for e in range(4):
                for d in (1, 2, 3):
                    at = quad(turn(third, 4 - d), turn(second, 4 - e))
                    arrive(at, 6 + (d - 1) * 4 + e)
                    push(at, twin, 18 + d * 4 + e)

        t_second = c * z + (1 - c) * x
        t_third = c * x + (1 - c) * y

        def stage5():
            for d in range(4):
                for e in range(4):
                    at = quad(turn(t_third, 4 - d), turn(t_second, 4 - e))
                    arrive_twin(at, 18 + d * 4 + e)

        return stage1, stage2, stage3, stage4, stage5

    s_stages = gather(states_out, sg_send, sg_recv)
    m_stages = gather(moments_out, mg_send, mg_recv)

    piece = part_s[rows]
    for n in range(15):
        out_s[n].wait_recv()
    for n in range(15):
        piece += land_s[n]
    states_out[c, own] = piece
    s_stages[0]()
    piece = part_m[rows]
    for n in range(15):
        out_m[n].wait_recv()
    for n in range(15):
        piece += land_m[n]
    moments_out[c, own] = piece.astype(BF16)
    m_stages[0]()
    for s, m in zip(s_stages[1:], m_stages[1:]):
        s()
        m()
    for copy in out_s + out_m + pending:
        copy.wait_send()


def gram_kernel(states_ref, moments_ref, gram_ref, rhs_ref, split, rates, row_feat):
    step = pl.program_id(0)
    rank, times = 128, split.shape[1]
    height, width = row_feat.shape[0], gram_ref.shape[1]

    def one_hot(base, count):
        k = lax.broadcasted_iota(jnp.int32, (count, rank), 0) + base
        t = lax.broadcasted_iota(jnp.int32, (count, rank), 1)
        start = rank + t * rank - lax.div(t * (t - 1), 2)
        quad_i = (k >= start) & (k < start + rank - t)
        offset = jnp.sum(jnp.where(quad_i, (t - start).astype(F32), 0.0), axis=1, keepdims=True)
        j = k + offset.astype(jnp.int32)
        linear = k < rank
        pick_i = jnp.where(quad_i | (linear & (t == k)), 1.0, 0.0).astype(BF16)
        pick_j = jnp.where((t == j) & (k >= rank), 1.0, 0.0).astype(BF16)
        plus = jnp.where(linear[:, :1], 1.0, 0.0)
        return jnp.concatenate([pick_i, pick_i], axis=1), jnp.concatenate([pick_j, pick_j], axis=1), plus

    def build(base, count):
        pick_i, pick_j, plus = one_hot(base, count)
        for n in range(times // 256):
            w = split[:, n * 256:(n + 1) * 256]
            a = jnp.dot(pick_i, w, preferred_element_type=F32)
            b = jnp.dot(pick_j, w, preferred_element_type=F32) + plus
            yield n, (a * b).astype(BF16)

    @pl.when(step == 0)
    def _():
        for g in range(8):
            gx, gz = g % 4, g // 4
            for b in range(8):
                y, z = b // 2, gz * 2 + b % 2
                at0 = (gx * 4 + z) * 4 + y
                at1 = (y * 4 + gx) * 4 + z
                s = jnp.concatenate([states_ref[0, at0], states_ref[1, at1]], axis=0)
                hi = s.astype(BF16)
                lo = (s - hi.astype(F32)).astype(BF16)
                cols = slice(g * 256, (g + 1) * 256)
                split[b * 16:(b + 1) * 16, cols] = hi
                split[rank + b * 16:rank + (b + 1) * 16, cols] = lo
                rates[b * 16:(b + 1) * 16, g * 256:g * 256 + 128] = moments_ref[0, at0]
                rates[b * 16:(b + 1) * 16, g * 256 + 128:(g + 1) * 256] = moments_ref[1, at1]
        for n, f in build(lax.axis_index("rows") * rhs_ref.shape[0], height):
            row_feat[:, n * 256:(n + 1) * 256] = f
        rhs = lax.dot_general(row_feat[...], rates[...], (((1,), (1,)), ((), ())), preferred_element_type=F32)
        rhs_ref[...] = rhs[:rhs_ref.shape[0]] * (1.0 / times)

    cols = [f for _, f in build(lax.axis_index("reg") * 1048 + step * width, width)]
    gram = lax.dot_general(
        row_feat[...], jnp.concatenate(cols, axis=1), (((1,), (1,)), ((), ())), preferred_element_type=F32
    )
    gram_ref[...] = gram[:gram_ref.shape[0]] * (1.0 / times)


def per_device(snapshots, rates, basis):
    n, t = snapshots.shape
    rank = basis.shape[1]
    assert rank == 128 and t == 256 and n % CHUNKS == 0
    assert lax.axis_size("rows") == 16 and lax.axis_size("reg") == 8
    width = rank + rank * (rank + 1) // 2
    dma = pltpu.SemaphoreType.DMA
    states, moments = pl.pallas_call(
        exchange_kernel,
        out_shape=(
            jax.ShapeDtypeStruct((2, 64, 8, 256), F32),
            jax.ShapeDtypeStruct((2, 64, 16, 128), BF16),
        ),
        in_specs=[pl.BlockSpec(memory_space=pl.ANY)] * 3,
        out_specs=[pl.BlockSpec(memory_space=pltpu.VMEM)] * 2,
        scratch_shapes=[
            pltpu.VMEM((n, t), BF16),
            pltpu.VMEM((n, t), BF16),
            pltpu.VMEM((n, rank), BF16),
            pltpu.VMEM((rank, n), BF16),
            pltpu.VMEM((16, 8, 256), F32),
            pltpu.VMEM((16, 16, 128), F32),
            pltpu.VMEM((15, 8, 256), F32),
            pltpu.VMEM((15, 16, 128), F32),
            dma((3, CHUNKS)),
            dma((15,)), dma((15,)), dma((15,)), dma((15,)),
            dma((34,)), dma((34,)), dma((34,)), dma((34,)),
        ],
        compiler_params=pltpu.CompilerParams(collective_id=0, has_side_effects=True, vmem_limit_bytes=32 << 20),
        name="exchange",
    )(snapshots, rates, basis)
    row_width, col_width = width // 16, width // 8
    return pl.pallas_call(
        gram_kernel,
        grid=(pl.cdiv(col_width, 256),),
        out_shape=(
            jax.ShapeDtypeStruct((row_width, col_width), F32),
            jax.ShapeDtypeStruct((row_width, rank), F32),
        ),
        in_specs=[
            pl.BlockSpec((2, 64, 8, 256), lambda i: (0, 0, 0, 0)),
            pl.BlockSpec((2, 64, 16, 128), lambda i: (0, 0, 0, 0)),
        ],
        out_specs=[
            pl.BlockSpec((row_width, 256), lambda i: (0, i)),
            pl.BlockSpec((row_width, rank), lambda i: (0, 0)),
        ],
        scratch_shapes=[
            pltpu.VMEM((2 * rank, 8 * t), BF16),
            pltpu.VMEM((rank, 8 * t), BF16),
            pltpu.VMEM((pl.cdiv(row_width, 16) * 16, 8 * t), BF16),
        ],
        compiler_params=pltpu.CompilerParams(vmem_limit_bytes=48 << 20),
        name="gram",
    )(states, moments)


def solution(mesh):
    return jax.shard_map(
        per_device,
        mesh=mesh,
        in_specs=(P("rows", "reg"), P("rows", "reg"), P("rows", None)),
        out_specs=(P("rows", "reg"), P("rows", None)),
        check_vma=False,
    )
```

time: 396 us -> 46.1 us (0.12)
  waiting for transfers between devices: 238 us -> 0 us
  blocking collectives: 53.6 us -> 0 us
  local copies, waits for them, and re-layouts: 50.7 us -> 5.96 us
  Pallas kernels: 0 us -> 39.3 us
  matrix products: 16.6 us -> 0 us
  starting transfers between devices: 14.2 us -> 0 us
  between operations: 13.9 us -> 0.65 us
  other arithmetic: 7.18 us -> 0 us
    psum x1 -> x0, waiting for transfers between devices: 118 us -> none  [per_device(): rhs = lax.psum(rhs_part, 'reg')]
    reduce_scatter x1 -> x0, waiting for transfers between devices: 60.6 us -> none  [per_device(): lax.psum_scatter(part_states, 'rows', scatter_dimension=1, tiled=True)]
    all_gather x2 -> x0, waiting for transfers between devices: 58.7 us -> none  [the longest x1 58.6 us: per_device(): lax.all_gather(row_feat, 'reg', axis=1, tiled=True)]
    psum x1 -> x0, blocking collectives: 53.6 us -> none  [per_device(): moments = lax.psum(part_rates, 'rows')]
    pallas_call x0 -> x2, Pallas kernels: none -> 39.3 us  [the longest x1 29.7 us: per_device(): pl.pallas_call(exchange_kernel, out_shape=(jax.ShapeDtypeStruct((2, 64, 8...]
    gather x2 -> x0, local copies, waits for them, and re-layouts: 32.7 us -> none  [make_features(): quad = jnp.take(states, upper_i, axis=0) * jnp.take(states, upper_j, axis=0)]
    dot_general x4 -> x0, matrix products: 16.6 us -> none  [the longest x1 8.04 us: block_adder(): lax.dot_general(piece, columns, (((1,), (1,)), ((), ())), preferred_eleme...]
    all_to_all x2 -> x0, starting transfers between devices: 14.1 us -> none  [the longest x1 7.54 us: per_device(): lax.all_to_all(local_feat, 'rows', split_axis=0, concat_axis=1, tiled=True)]
  transfers between devices with their start and end apart: 6 -> 0, of which waited for: 3 -> 0; matrix products, arithmetic and copies ran while one was open for 5% -> 0% of each run, Pallas kernels for 0% -> 0%
where the time goes in v1:
time: 46.1 us; the launch traced here: 45.9 us
  Pallas kernels  39.3 us (85%)
  local copies, waits for them, and re-layouts  5.96 us (13%)
  between operations  0.65 us (1%)
    pallas_call x1, Pallas kernels, per_device(): pl.pallas_call(exchange_kernel, out_shape=(jax.ShapeDtypeStruct((2, 64, 8...  29.7 us
    pallas_call x1, Pallas kernels, per_device(): pl.pallas_call(gram_kernel, grid=(pl.cdiv(col_width, 256),), out_shape=(j...  9.64 us
    unnamed x6, local copies, waits for them, and re-layouts  5.96 us

profile of v1, /device:TPU:1, one launch (start us, length us, event | category | flops | bytes accessed | tf_op | source)
XLA Modules:
  0.0 45.9 jit_solution(8199456569116421746)
XLA Ops:
  0.6 0.0 copy-start
  0.6 2.2 %copy-done = bf16[8192,256]{1,0:T(8,128)(2,1)S(1)} copy-done((bf16[8192,256]{1,0:T(8,128)(2,1)S(1)}, bf16[8192,256]{1,0:T(8,128)(2,1)}, u32[]{:S(2)}) %copy-start) | copy-done | bytes 4194328
  2.8 0.0 copy-start.1
  2.8 2.2 %copy-done.1 = bf16[8192,256]{1,0:T(8,128)(2,1)S(1)} copy-done((bf16[8192,256]{1,0:T(8,128)(2,1)S(1)}, bf16[8192,256]{1,0:T(8,128)(2,1)}, u32[]{:S(2)}) %copy-start.1) | copy-done | bytes 4194328
  5.0 0.0 copy-start.2
  5.0 1.6 %copy-done.2 = bf16[8192,128]{1,0:T(8,128)(2,1)S(1)} copy-done((bf16[8192,128]{1,0:T(8,128)(2,1)S(1)}, bf16[8192,128]{1,0:T(8,128)(2,1)}, u32[]{:S(2)}) %copy-start.2) | copy-done | bytes 2097176
  6.6 29.7 %exchange.1 = (f32[2,64,8,256]{3,2,1,0:T(8,128)S(1)}, bf16[2,64,16,128]{3,2,1,0:T(8,128)(2,1)S(1)}) custom-call(bf16[8192,256]{1,0:T(8,128)(2,1)S(1)} %copy-done, bf16[8192,256]{1,0:T(8,128)(2,1)S(1)} %copy-done.1, bf16[8192,128]{1,0:T(8,128)(2,1)S(1)} %copy-done.2), custom_call_target="tpu_custom_call" | custom-call | tf_op jit(solution)/shard_map/exchange/pallas_call | solution.py:265
  36.3 9.6 %gram.1 = (f32[524,1048]{1,0:T(8,128)}, f32[524,128]{1,0:T(8,128)}) custom-call(f32[2,64,8,256]{3,2,1,0:T(8,128)S(1)} %get-tuple-element.4.states_ref, bf16[2,64,16,128]{3,2,1,0:T(8,128)(2,1)S(1)} %get-tuple-element.5.moments_ref), custom_call_target="tpu_custom_call" | custom-call | tf_op jit(solution)/shard_map/gram/pallas_call | solution.py:290
Async XLA Ops:
  0.6 2.2 %copy-start = (bf16[8192,256]{1,0:T(8,128)(2,1)S(1)}, bf16[8192,256]{1,0:T(8,128)(2,1)}, u32[]{:S(2)}) copy-start(bf16[8192,256]{1,0:T(8,128)(2,1)} %snap_hbm.1) | copy-start | bytes 12582916
  2.8 2.2 %copy-start.1 = (bf16[8192,256]{1,0:T(8,128)(2,1)S(1)}, bf16[8192,256]{1,0:T(8,128)(2,1)}, u32[]{:S(2)}) copy-start(bf16[8192,256]{1,0:T(8,128)(2,1)} %rates_hbm.1) | copy-start | bytes 12582916
  5.0 1.6 %copy-start.2 = (bf16[8192,128]{1,0:T(8,128)(2,1)S(1)}, bf16[8192,128]{1,0:T(8,128)(2,1)}, u32[]{:S(2)}) copy-start(bf16[8192,128]{1,0:T(8,128)(2,1)} %basis_hbm.1) | copy-start | bytes 6291460

commit v2 on v0

v2 whole, which is shorter than its diff:
```python
import jax
import jax.numpy as jnp
from jax import lax
from jax.experimental import pallas as pl
from jax.experimental.pallas import tpu as pltpu
from jax.sharding import PartitionSpec as P

MESH = pl.DeviceIdType.MESH
F32 = jnp.float32
BF16 = jnp.bfloat16
CHUNKS = 4
VMEM_KIB = 47000


def device_at(x, y, z, c):
    return ((y * 2 + lax.rem(z, 2)) * 2 + c, lax.div(z, 2) * 4 + x)


def one_hot(base, count):
    rank = 128
    k = lax.broadcasted_iota(jnp.int32, (count, rank), 0) + base
    t = lax.broadcasted_iota(jnp.int32, (count, rank), 1)
    start = rank + t * rank - lax.div(t * (t - 1), 2)
    quad_i = (k >= start) & (k < start + rank - t)
    offset = jnp.sum(jnp.where(quad_i, t - start, 0).astype(F32), axis=1, keepdims=True)
    linear = k < rank
    pick_i = jnp.where(quad_i | (linear & (t == k)), 1.0, 0.0).astype(BF16)
    pick_j = jnp.where(((t - k).astype(F32) == offset) & (k >= rank), 1.0, 0.0).astype(BF16)
    return pick_i, pick_j


def exchange_kernel(
    snap_hbm, rates_hbm, basis_hbm, gram_out, row_out, moments_out,
    states, moments, row_feat, col_feat, acc, gram, snap, rates, basis, basis_t, part_s, part_m, land_s, land_m, pick_i, pick_j,
    load_sem, send_s, recv_s, send_m, recv_m,
    sg_send, sg_recv, mg_send, mg_recv, out_sem,
):
    rows, reg = lax.axis_index("rows"), lax.axis_index("reg")
    c = lax.rem(rows, 2)
    zl = lax.rem(lax.div(rows, 2), 2)
    y = lax.div(rows, 4)
    x = lax.rem(reg, 4)
    zh = lax.div(reg, 4)
    z = zh * 2 + zl
    twin = device_at(x, y, z, 1 - c)

    def turn(v, d):
        return lax.rem(v + d, 4)

    group = [(dy, dz, dc) for dy in range(4) for dz in range(2) for dc in range(2)][1:]

    def group_row(dy, dz, dc):
        return (turn(y, dy) * 2 + lax.rem(zl + dz, 2)) * 2 + lax.rem(c + dc, 2)

    depth = snap_hbm.shape[0] // CHUNKS
    loads = {}
    for i, k in [(i, k) for k in range(CHUNKS) for i in (0, 1)] + [(2, k) for k in range(CHUNKS)]:
        at = pl.ds(k * depth, depth)
        src, dst = ((basis_hbm, basis), (snap_hbm, snap), (rates_hbm, rates))[i]
        loads[i, k] = pltpu.make_async_copy(src.at[at, :], dst.at[at, :], load_sem.at[i, k])
        loads[i, k].start()

    barrier = pltpu.get_barrier_semaphore()
    with jax.named_scope("signal"):
        for dy, dz, dc in group:
            pl.semaphore_signal(barrier, inc=1, device_id=(group_row(dy, dz, dc), reg), device_id_type=MESH)
        for d in (1, 2, 3):
            pl.semaphore_signal(barrier, inc=1, device_id=device_at(turn(x, d), y, z, c), device_id_type=MESH)
        for d in (2, 3 + 2 * zl):
            pl.semaphore_signal(barrier, inc=1, device_id=device_at(x, y, turn(z, d), c), device_id_type=MESH)

    def all_of(ref, send, recv):
        return pltpu.make_async_remote_copy(
            src_ref=ref, dst_ref=ref, send_sem=send, recv_sem=recv, device_id=twin, device_id_type=MESH
        )

    def scatter(part, land, send, recv):
        for n, (dy, dz, dc) in enumerate(group):
            to = group_row(dy, dz, dc)
            pltpu.make_async_remote_copy(
                src_ref=part.at[to], dst_ref=land.at[n], send_sem=send, recv_sem=recv,
                device_id=(to, reg), device_id_type=MESH,
            ).start()

    def collect(part, land, send, recv):
        all_of(land, send, recv).wait_recv()
        piece = part[rows]
        for n in range(15):
            piece += land[n]
        return piece

    with jax.named_scope("proj_s"):
        total = jnp.zeros((128, 256), F32)
        for k in range(CHUNKS):
            at = pl.ds(k * depth, depth)
            loads[0, k].wait()
            loads[1, k].wait()
            turned = basis[at, :].T
            basis_t[:, at] = turned
            total += jnp.dot(turned, snap[at, :], preferred_element_type=F32)
        part_s[...] = total.T.reshape(16, 16, 128)
    with jax.named_scope("barrier_wait"):
        pl.semaphore_wait(barrier, 20)
    with jax.named_scope("send_s"):
        scatter(part_s, land_s, send_s, recv_s)
    with jax.named_scope("proj_m"):
        total = jnp.zeros((128, 256), F32)
        for k in range(CHUNKS):
            at = pl.ds(k * depth, depth)
            loads[2, k].wait()
            total += jnp.dot(basis_t[:, at], rates[at, :], preferred_element_type=F32)
        part_m[...] = total.T.reshape(16, 16, 128)
    with jax.named_scope("send_m"):
        scatter(part_m, land_m, send_m, recv_m)

    height, width = row_feat.shape[0], col_feat.shape[0]
    row_base, col_base = rows * 524, reg * 1048
    with jax.named_scope("picks"):
        for at, base, count in ((0, row_base, height), (height, col_base, width)):
            pick_i[at:at + count, :], pick_j[at:at + count, :] = one_hot(base, count)

    first = (1 - c) * y + c * z
    second = (1 - c) * z + c * x
    third = (1 - c) * x + c * y
    t_second = c * z + (1 - c) * x
    t_third = c * x + (1 - c) * y

    def peer(stage, d):
        step0, step1 = (1 - c) * d, c * d
        if stage == 1:
            return device_at(x, turn(y, step0), turn(z, step1), c)
        if stage == 2:
            return device_at(turn(x, step1), y, turn(z, step0), c)
        return device_at(turn(x, step0), turn(y, step1), z, c)

    own = (third * 4 + second) * 4 + first

    def quad(a3, a2):
        return pl.ds((a3 * 4 + a2) * 4, 4)

    def gather(buf, send, recv):
        flat = buf.reshape(128, *buf.shape[2:])

        def push(at, device, n):
            pltpu.make_async_remote_copy(
                src_ref=buf.at[c, at], dst_ref=buf.at[c, at], send_sem=send, recv_sem=recv.at[n],
                device_id=device, device_id_type=MESH,
            ).start()

        def arrive(core, at, n):
            all_of(buf.at[core, at], send, recv.at[n]).wait_recv()

        def stage1():
            for d in (1, 3, 2):
                push(pl.ds(own, 1), peer(1, d), 0)

        def stage2():
            arrive(c, pl.ds(0, 3), 0)
            mine = quad(third, second)
            for d in (2, 1, 3):
                push(mine, peer(2, d), d)
            for d in (1, 3, 2):
                push(mine, peer(3, d), 3 + d)

        def stage3():
            for e in (1, 3, 2):
                at = quad(third, turn(second, 4 - e))
                arrive(c, at, e)
                for d in (2, 1, 3):
                    push(at, peer(3, d), 3 + d)
            push(pl.ds(third * 16, 16), twin, 7)

        def from_afar(d):
            at = pl.ds(turn(third, 4 - d) * 16, 16)
            arrive(c, at, 3 + d)
            push(at, twin, 7 + d)

        def from_twin(d):
            arrive(1 - c, pl.ds(turn(t_third, 4 - d) * 16, 16), 7 + d)

        def drain():
            all_of(flat.at[pl.ds(0, 127)], send, recv.at[0]).wait_send()

        return stage1, stage2, stage3, from_afar, from_twin, drain

    s1, s2, s3, s_afar, s_twin, s_drain = gather(states, sg_send, sg_recv)
    m1, m2, m3, m_afar, m_twin, m_drain = gather(moments, mg_send, mg_recv)

    def features(core, a3, n):
        s = states[core, pl.ds(a3 * 16, 16)].reshape(256, 128)
        hi = s.astype(BF16)
        lo = (s - hi.astype(F32)).astype(BF16)
        split = jnp.concatenate([hi, lo], axis=1)

        def select(pick, at, count):
            e = pick[at:at + count, :]
            return lax.dot_general(
                jnp.concatenate([e, e], axis=1), split, (((1,), (1,)), ((), ())), preferred_element_type=F32
            )

        for out, at, base, slot in ((row_feat, 0, row_base, n), (col_feat, height, col_base, n % 2)):
            cols = slice(slot * 256, (slot + 1) * 256)
            k = lax.broadcasted_iota(jnp.int32, (128, 256), 0) + base
            plus = jnp.where(k < 128, 1.0, 0.0)
            count = out.shape[0]
            a, b = select(pick_i, at, count), select(pick_j, at, count)
            out[:128, cols] = (a[:128] * (b[:128] + plus)).astype(BF16)
            out[128:, cols] = (a[128:] * b[128:]).astype(BF16)
        cols = slice(n * 256, (n + 1) * 256)
        pltpu.make_async_copy(row_feat.at[:, cols], row_out.at[:, cols], out_sem.at[0]).start()

    times = row_feat.shape[1]
    out_rows, out_cols = gram.shape
    outs = [(row_feat, row_out, 0), (gram, gram_out, 1), (moments, moments_out, 2)]

    def accumulate(pair):
        lhs = row_feat[:, pair * 512:(pair + 1) * 512]
        for at in range(0, width, 256):
            to = min(at + 256, width)
            part = lax.dot_general(
                lhs, col_feat[at:to, :], (((1,), (1,)), ((), ())), preferred_element_type=F32
            )
            if pair:
                part += acc[:, at:to]
            if pair < times // 512 - 1:
                acc[:, at:to] = part
            else:
                to = min(to, out_cols)
                gram[:, at:to] = part[:out_rows, :to - at] * (1.0 / times)

    with jax.named_scope("rs_s"):
        states[c, own] = collect(part_s, land_s, send_s, recv_s)
    s1()
    with jax.named_scope("s2"):
        s2()
    with jax.named_scope("s3"):
        s3()
    with jax.named_scope("rs_m"):
        moments[c, own] = collect(part_m, land_m, send_m, recv_m).astype(BF16)
        m1()
    for n, d in enumerate((0, 1, 3, 2)):
        if d:
            with jax.named_scope(f"a{n}"):
                s_afar(d)
        with jax.named_scope(f"fa{n}"):
            features(c, turn(third, 4 - d), 2 * n)
        with jax.named_scope(f"t{n}"):
            s_twin(d)
        with jax.named_scope(f"ft{n}"):
            features(1 - c, turn(t_third, 4 - d), 2 * n + 1)
        with jax.named_scope(f"m{n}"):
            (m2, m3, lambda: m_afar(1), lambda: [m_afar(3), m_afar(2)])[n]()
        with jax.named_scope(f"g{n}"):
            accumulate(n)
    pltpu.make_async_copy(gram, gram_out, out_sem.at[1]).start()
    with jax.named_scope("m_twin"):
        for d in range(4):
            m_twin(d)
    pltpu.make_async_copy(moments, moments_out, out_sem.at[2]).start()
    with jax.named_scope("drain"):
        all_of(land_s, send_s, recv_s).wait_send()
        all_of(land_m, send_m, recv_m).wait_send()
        s_drain()
        m_drain()
        for src, dst, n in outs:
            pltpu.make_async_copy(src, dst, out_sem.at[n]).wait()


def finish_kernel(gram_ref, row_ref, moments_ref, gram_out, rhs_out, rhs_ref, sem):
    copy = pltpu.make_async_copy(gram_ref, gram_out, sem.at[0])
    copy.start()
    times = row_ref.shape[1]
    rows, reg = lax.axis_index("rows"), lax.axis_index("reg")
    c = lax.rem(rows, 2)
    y, x = lax.div(rows, 4), lax.rem(reg, 4)
    blocks = []
    for n, (d, far) in enumerate((d, far) for d in (0, 1, 3, 2) for far in (0, 1)):
        core = lax.rem(c + far, 2)
        a3 = lax.rem((1 - core) * x + core * y + 4 - d, 4)
        blocks.append(moments_ref[core, pl.ds(a3 * 16, 16)].reshape(256, 128))
    with jax.named_scope("rhs"):
        rhs = jnp.dot(row_ref[...], jnp.concatenate(blocks, axis=0), preferred_element_type=F32)
        rhs_ref[...] = rhs[:rhs_ref.shape[0]] * (1.0 / times)
    with jax.named_scope("k2wait"):
        rhs_copy = pltpu.make_async_copy(rhs_ref, rhs_out, sem.at[1])
        rhs_copy.start()
        copy.wait()
        rhs_copy.wait()


def per_device(snapshots, rates, basis):
    n, t = snapshots.shape
    rank = basis.shape[1]
    width = rank + rank * (rank + 1) // 2
    assert rank == 128 and t == 256 and n % CHUNKS == 0
    assert lax.axis_size("rows") == 16 and lax.axis_size("reg") == 8
    row_width, col_width = width // 16, width // 8
    row_pad, col_pad = pl.cdiv(row_width, 16) * 16, pl.cdiv(col_width, 16) * 16
    dma = pltpu.SemaphoreType.DMA
    gram, row_feat, moments = pl.pallas_call(
        exchange_kernel,
        out_shape=(
            jax.ShapeDtypeStruct((row_width, col_width), F32),
            jax.ShapeDtypeStruct((row_pad, 8 * t), BF16),
            jax.ShapeDtypeStruct((2, 64, 16, rank), BF16),
        ),
        in_specs=[pl.BlockSpec(memory_space=pl.ANY)] * 3,
        out_specs=[pl.BlockSpec(memory_space=pl.ANY)] * 3,
        scratch_shapes=[
            pltpu.VMEM((2, 64, 16, rank), F32),
            pltpu.VMEM((2, 64, 16, rank), BF16),
            pltpu.VMEM((row_pad, 8 * t), BF16),
            pltpu.VMEM((col_pad, 2 * t), BF16),
            pltpu.VMEM((row_pad, col_pad), F32),
            pltpu.VMEM((row_width, col_width), F32),
            pltpu.VMEM((n, t), BF16),
            pltpu.VMEM((n, t), BF16),
            pltpu.VMEM((n, rank), BF16),
            pltpu.VMEM((rank, n), BF16),
            pltpu.VMEM((16, 16, rank), F32),
            pltpu.VMEM((16, 16, rank), F32),
            pltpu.VMEM((15, 16, rank), F32),
            pltpu.VMEM((15, 16, rank), F32),
            pltpu.VMEM((row_pad + col_pad, rank), BF16),
            pltpu.VMEM((row_pad + col_pad, rank), BF16),
            dma((3, CHUNKS)),
            dma, dma, dma, dma,
            dma, dma((11,)), dma, dma((11,)), dma((3,)),
        ],
        compiler_params=pltpu.CompilerParams(
            collective_id=0, has_side_effects=True, vmem_limit_bytes=VMEM_KIB << 10
        ),
        name="exchange",
    )(*[pltpu.with_memory_space_constraint(a, pltpu.MemorySpace.HBM) for a in (snapshots, rates, basis)])
    return pl.pallas_call(
        finish_kernel,
        out_shape=(
            jax.ShapeDtypeStruct((row_width, col_width), F32),
            jax.ShapeDtypeStruct((row_width, rank), F32),
        ),
        in_specs=[
            pl.BlockSpec(memory_space=pl.ANY),
            pl.BlockSpec(memory_space=pltpu.VMEM),
            pl.BlockSpec(memory_space=pltpu.VMEM),
        ],
        out_specs=[pl.BlockSpec(memory_space=pl.ANY)] * 2,
        scratch_shapes=[pltpu.VMEM((row_width, rank), F32), dma((2,))],
        compiler_params=pltpu.CompilerParams(vmem_limit_bytes=16 << 20),
        name="finish",
    )(gram, row_feat, moments)


def solution(mesh):
    return jax.shard_map(
        per_device,
        mesh=mesh,
        in_specs=(P("rows", "reg"), P("rows", "reg"), P("rows", None)),
        out_specs=(P("rows", "reg"), P("rows", None)),
        check_vma=False,
    )
```

time: 396 us -> 38.8 us (0.10)
  waiting for transfers between devices: 238 us -> 0 us
  blocking collectives: 53.6 us -> 0 us
  local copies, waits for them, and re-layouts: 50.7 us -> 0 us
  Pallas kernels: 0 us -> 38 us
  matrix products: 16.6 us -> 0 us
  starting transfers between devices: 14.2 us -> 0 us
  between operations: 13.9 us -> 0.64 us
  other arithmetic: 7.18 us -> 0 us
    psum x1 -> x0, waiting for transfers between devices: 118 us -> none  [per_device(): rhs = lax.psum(rhs_part, 'reg')]
    reduce_scatter x1 -> x0, waiting for transfers between devices: 60.6 us -> none  [per_device(): lax.psum_scatter(part_states, 'rows', scatter_dimension=1, tiled=True)]
    all_gather x2 -> x0, waiting for transfers between devices: 58.7 us -> none  [the longest x1 58.6 us: per_device(): lax.all_gather(row_feat, 'reg', axis=1, tiled=True)]
    psum x1 -> x0, blocking collectives: 53.6 us -> none  [per_device(): moments = lax.psum(part_rates, 'rows')]
    pallas_call x0 -> x2, Pallas kernels: none -> 38 us  [the longest x1 36.2 us: per_device(): pl.pallas_call(exchange_kernel, out_shape=(jax.ShapeDtypeStruct((row_widt...]
    gather x2 -> x0, local copies, waits for them, and re-layouts: 32.7 us -> none  [make_features(): quad = jnp.take(states, upper_i, axis=0) * jnp.take(states, upper_j, axis=0)]
    dot_general x4 -> x0, matrix products: 16.6 us -> none  [the longest x1 8.04 us: block_adder(): lax.dot_general(piece, columns, (((1,), (1,)), ((), ())), preferred_eleme...]
    all_to_all x2 -> x0, starting transfers between devices: 14.1 us -> none  [the longest x1 7.54 us: per_device(): lax.all_to_all(local_feat, 'rows', split_axis=0, concat_axis=1, tiled=True)]
  transfers between devices with their start and end apart: 6 -> 0, of which waited for: 3 -> 0; matrix products, arithmetic and copies ran while one was open for 5% -> 0% of each run, Pallas kernels for 0% -> 0%
where the time goes in v2:
time: 38.8 us; the launch traced here: 38.7 us
  Pallas kernels  38 us (98%)
  between operations  0.64 us (2%)
    pallas_call x1, Pallas kernels, per_device(): pl.pallas_call(exchange_kernel, out_shape=(jax.ShapeDtypeStruct((row_widt...  36.2 us
    pallas_call x1, Pallas kernels, per_device(): pl.pallas_call(finish_kernel, out_shape=(jax.ShapeDtypeStruct((row_width,...  1.78 us

profile of v2, /device:TPU:1, one launch (start us, length us, event | category | flops | bytes accessed | tf_op | source)
XLA Modules:
  0.0 38.7 jit_solution(15377806765375800298)
XLA Ops:
  0.6 36.2 %exchange.1 = (f32[524,1048]{1,0:T(8,128)S(1)}, bf16[528,2048]{1,0:T(8,128)(2,1)S(1)}, bf16[2,64,16,128]{3,2,1,0:T(8,128)(2,1)S(1)}) custom-call(bf16[8192,256]{1,0:T(8,128)(2,1)} %snap_hbm.1, bf16[8192,256]{1,0:T(8,128)(2,1)} %rates_hbm.1, bf16[8192,128]{1,0:T(8,128)(2,1)} %basis_hbm.1), custom_call_target="tpu_custom_call" | custom-call | tf_op jit(solution)/shard_map/exchange/pallas_call | solution.py:300
  36.9 1.8 %finish.1 = (f32[524,1048]{1,0:T(8,128)}, f32[524,128]{1,0:T(8,128)}) custom-call(f32[524,1048]{1,0:T(8,128)S(1)} %get-tuple-element.5.gram_ref, bf16[528,2048]{1,0:T(8,128)(2,1)S(1)} %get-tuple-element.6.row_ref, bf16[2,64,16,128]{3,2,1,0:T(8,128)(2,1)S(1)} %get-tuple-element.7.moments_ref), custom_call_target="tpu_custom_call" | custom-call | tf_op jit(solution)/shard_map/finish/pallas_call | solution.py:335

commit v3 on v2

--- a/solution.py
+++ b/solution.py
@@ -48,9 +48,17 @@
         return lax.rem(v + d, 4)
 
     group = [(dy, dz, dc) for dy in range(4) for dz in range(2) for dc in range(2)][1:]
+    chips = sorted(
+        ((dx, dy, dz) for dx in range(4) for dy in range(4) for dz in range(4)),
+        key=lambda d: (sum(min(a, 4 - a) for a in d), d),
+    )
+    xs, ys, zs = ([turn(v, d) for d in range(4)] for v in (x, y, z))
 
     def group_row(dy, dz, dc):
-        return (turn(y, dy) * 2 + lax.rem(zl + dz, 2)) * 2 + lax.rem(c + dc, 2)
+        return (ys[dy] * 2 + lax.rem(zl + dz, 2)) * 2 + lax.rem(c + dc, 2)
+
+    def chip(dx, dy, dz):
+        return device_at(xs[dx], ys[dy], zs[dz], c)
 
     depth = snap_hbm.shape[0] // CHUNKS
     loads = {}
@@ -63,11 +71,10 @@
     barrier = pltpu.get_barrier_semaphore()
     with jax.named_scope("signal"):
         for dy, dz, dc in group:
-            pl.semaphore_signal(barrier, inc=1, device_id=(group_row(dy, dz, dc), reg), device_id_type=MESH)
-        for d in (1, 2, 3):
-            pl.semaphore_signal(barrier, inc=1, device_id=device_at(turn(x, d), y, z, c), device_id_type=MESH)
-        for d in (2, 3 + 2 * zl):
-            pl.semaphore_signal(barrier, inc=1, device_id=device_at(x, y, turn(z, d), c), device_id_type=MESH)
+            if dc:
+                pl.semaphore_signal(barrier, inc=1, device_id=(group_row(dy, dz, dc), reg), device_id_type=MESH)
+        for d in chips[1:]:
+            pl.semaphore_signal(barrier, inc=1, device_id=chip(*d), device_id_type=MESH)
 
     def all_of(ref, send, recv):
         return pltpu.make_async_remote_copy(
@@ -100,7 +107,7 @@
             total += jnp.dot(turned, snap[at, :], preferred_element_type=F32)
         part_s[...] = total.T.reshape(16, 16, 128)
     with jax.named_scope("barrier_wait"):
-        pl.semaphore_wait(barrier, 20)
+        pl.semaphore_wait(barrier, 71)
     with jax.named_scope("send_s"):
         scatter(part_s, land_s, send_s, recv_s)
     with jax.named_scope("proj_m"):
@@ -119,75 +126,37 @@
         for at, base, count in ((0, row_base, height), (height, col_base, width)):
             pick_i[at:at + count, :], pick_j[at:at + count, :] = one_hot(base, count)
 
-    first = (1 - c) * y + c * z
-    second = (1 - c) * z + c * x
-    third = (1 - c) * x + c * y
-    t_second = c * z + (1 - c) * x
-    t_third = c * x + (1 - c) * y
-
-    def peer(stage, d):
-        step0, step1 = (1 - c) * d, c * d
-        if stage == 1:
-            return device_at(x, turn(y, step0), turn(z, step1), c)
-        if stage == 2:
-            return device_at(turn(x, step1), y, turn(z, step0), c)
-        return device_at(turn(x, step0), turn(y, step1), z, c)
-
-    own = (third * 4 + second) * 4 + first
-
-    def quad(a3, a2):
-        return pl.ds((a3 * 4 + a2) * 4, 4)
-
     def gather(buf, send, recv):
         flat = buf.reshape(128, *buf.shape[2:])
 
-        def push(at, device, n):
+        def scatter_out():
+            for n, d in enumerate(chips[1:], 1):
+                pltpu.make_async_remote_copy(
+                    src_ref=buf.at[c, 0], dst_ref=buf.at[c, n], send_sem=send, recv_sem=recv.at[n // 16],
+                    device_id=chip(*d), device_id_type=MESH,
+                ).start()
+
+        def arrive(n):
+            at = pl.ds(n * 16, 16)
+            all_of(buf.at[c, pl.ds(0, 15) if n == 0 else at], send, recv.at[n]).wait_recv()
             pltpu.make_async_remote_copy(
-                src_ref=buf.at[c, at], dst_ref=buf.at[c, at], send_sem=send, recv_sem=recv.at[n],
-                device_id=device, device_id_type=MESH,
+                src_ref=buf.at[c, at], dst_ref=buf.at[c, at], send_sem=send, recv_sem=recv.at[4 + n],
+                device_id=twin, device_id_type=MESH,
             ).start()
 
-        def arrive(core, at, n):
-            all_of(buf.at[core, at], send, recv.at[n]).wait_recv()
-
-        def stage1():
-            for d in (1, 3, 2):
-                push(pl.ds(own, 1), peer(1, d), 0)
-
-        def stage2():
-            arrive(c, pl.ds(0, 3), 0)
-            mine = quad(third, second)
-            for d in (2, 1, 3):
-                push(mine, peer(2, d), d)
-            for d in (1, 3, 2):
-                push(mine, peer(3, d), 3 + d)
-
-        def stage3():
-            for e in (1, 3, 2):
-                at = quad(third, turn(second, 4 - e))
-                arrive(c, at, e)
-                for d in (2, 1, 3):
-                    push(at, peer(3, d), 3 + d)
-            push(pl.ds(third * 16, 16), twin, 7)
-
-        def from_afar(d):
-            at = pl.ds(turn(third, 4 - d) * 16, 16)
-            arrive(c, at, 3 + d)
-            push(at, twin, 7 + d)
-
-        def from_twin(d):
-            arrive(1 - c, pl.ds(turn(t_third, 4 - d) * 16, 16), 7 + d)
+        def from_twin(n):
+            all_of(buf.at[1 - c, pl.ds(n * 16, 16)], send, recv.at[4 + n]).wait_recv()
 
         def drain():
             all_of(flat.at[pl.ds(0, 127)], send, recv.at[0]).wait_send()
 
-        return stage1, stage2, stage3, from_afar, from_twin, drain
-
-    s1, s2, s3, s_afar, s_twin, s_drain = gather(states, sg_send, sg_recv)
-    m1, m2, m3, m_afar, m_twin, m_drain = gather(moments, mg_send, mg_recv)
-
-    def features(core, a3, n):
-        s = states[core, pl.ds(a3 * 16, 16)].reshape(256, 128)
+        return scatter_out, arrive, from_twin, drain
+
+    s_out, s_arrive, s_twin, s_drain = gather(states, sg_send, sg_recv)
+    m_out, m_arrive, m_twin, m_drain = gather(moments, mg_send, mg_recv)
+
+    def features(core, block, n):
+        s = states[core, block * 16:(block + 1) * 16].reshape(256, 128)
         hi = s.astype(BF16)
         lo = (s - hi.astype(F32)).astype(BF16)
         split = jnp.concatenate([hi, lo], axis=1)
@@ -229,33 +198,35 @@
                 gram[:, at:to] = part[:out_rows, :to - at] * (1.0 / times)
 
     with jax.named_scope("rs_s"):
-        states[c, own] = collect(part_s, land_s, send_s, recv_s)
-    s1()
-    with jax.named_scope("s2"):
-        s2()
-    with jax.named_scope("s3"):
-        s3()
+        states[c, 0] = collect(part_s, land_s, send_s, recv_s)
+    with jax.named_scope("s_out"):
+        s_out()
     with jax.named_scope("rs_m"):
-        moments[c, own] = collect(part_m, land_m, send_m, recv_m).astype(BF16)
-        m1()
-    for n, d in enumerate((0, 1, 3, 2)):
-        if d:
-            with jax.named_scope(f"a{n}"):
-                s_afar(d)
+        moments[c, 0] = collect(part_m, land_m, send_m, recv_m).astype(BF16)
+    with jax.named_scope("m_out"):
+        m_out()
+    with jax.named_scope("a0"):
+        s_arrive(0)
+    for n in range(4):
         with jax.named_scope(f"fa{n}"):
-            features(c, turn(third, 4 - d), 2 * n)
+            features(c, n, 2 * n)
+        if n < 3:
+            with jax.named_scope(f"a{n + 1}"):
+                s_arrive(n + 1)
+        else:
+            with jax.named_scope("m_arrive"):
+                for k in range(4):
+                    m_arrive(k)
         with jax.named_scope(f"t{n}"):
-            s_twin(d)
+            s_twin(n)
         with jax.named_scope(f"ft{n}"):
-            features(1 - c, turn(t_third, 4 - d), 2 * n + 1)
-        with jax.named_scope(f"m{n}"):
-            (m2, m3, lambda: m_afar(1), lambda: [m_afar(3), m_afar(2)])[n]()
+            features(1 - c, n, 2 * n + 1)
         with jax.named_scope(f"g{n}"):
             accumulate(n)
     pltpu.make_async_copy(gram, gram_out, out_sem.at[1]).start()
     with jax.named_scope("m_twin"):
-        for d in range(4):
-            m_twin(d)
+        for k in range(4):
+            m_twin(k)
     pltpu.make_async_copy(moments, moments_out, out_sem.at[2]).start()
     with jax.named_scope("drain"):
         all_of(land_s, send_s, recv_s).wait_send()
@@ -270,14 +241,8 @@
     copy = pltpu.make_async_copy(gram_ref, gram_out, sem.at[0])
     copy.start()
     times = row_ref.shape[1]
-    rows, reg = lax.axis_index("rows"), lax.axis_index("reg")
-    c = lax.rem(rows, 2)
-    y, x = lax.div(rows, 4), lax.rem(reg, 4)
-    blocks = []
-    for n, (d, far) in enumerate((d, far) for d in (0, 1, 3, 2) for far in (0, 1)):
-        core = lax.rem(c + far, 2)
-        a3 = lax.rem((1 - core) * x + core * y + 4 - d, 4)
-        blocks.append(moments_ref[core, pl.ds(a3 * 16, 16)].reshape(256, 128))
+    c = lax.rem(lax.axis_index("rows"), 2)
+    blocks = [moments_ref[core, n * 16:(n + 1) * 16].reshape(256, 128) for n in range(4) for core in (c, 1 - c)]
     with jax.named_scope("rhs"):
         rhs = jnp.dot(row_ref[...], jnp.concatenate(blocks, axis=0), preferred_element_type=F32)
         rhs_ref[...] = rhs[:rhs_ref.shape[0]] * (1.0 / times)
@@ -325,7 +290,7 @@
             pltpu.VMEM((row_pad + col_pad, rank), BF16),
             dma((3, CHUNKS)),
             dma, dma, dma, dma,
-            dma, dma((11,)), dma, dma((11,)), dma((3,)),
+            dma, dma((8,)), dma, dma((8,)), dma((3,)),
         ],
         compiler_params=pltpu.CompilerParams(
             collective_id=0, has_side_effects=True, vmem_limit_bytes=VMEM_KIB << 10

time: 38.8 us -> 33.4 us (0.86)
  Pallas kernels: 38 us -> 32.6 us
    pallas_call x1, Pallas kernels: 36.2 us -> 31.1 us  [per_device(): pl.pallas_call(exchange_kernel, out_shape=(jax.ShapeDtypeStruct((row_widt...]
where the time goes in v3:
time: 33.4 us; the launch traced here: 33.2 us
  Pallas kernels  32.6 us (98%)
  between operations  0.64 us (2%)
    pallas_call x1, Pallas kernels, per_device(): pl.pallas_call(exchange_kernel, out_shape=(jax.ShapeDtypeStruct((row_widt...  31.1 us
    pallas_call x1, Pallas kernels, per_device(): pl.pallas_call(finish_kernel, out_shape=(jax.ShapeDtypeStruct((row_width,...  1.54 us

profile of v3, /device:TPU:1, one launch (start us, length us, event | category | flops | bytes accessed | tf_op | source)
XLA Modules:
  0.0 33.2 jit_solution(9898252533421209473)
XLA Ops:
  0.6 31.1 %exchange.1 = (f32[524,1048]{1,0:T(8,128)S(1)}, bf16[528,2048]{1,0:T(8,128)(2,1)S(1)}, bf16[2,64,16,128]{3,2,1,0:T(8,128)(2,1)S(1)}) custom-call(bf16[8192,256]{1,0:T(8,128)(2,1)} %snap_hbm.1, bf16[8192,256]{1,0:T(8,128)(2,1)} %rates_hbm.1, bf16[8192,128]{1,0:T(8,128)(2,1)} %basis_hbm.1), custom_call_target="tpu_custom_call" | custom-call | tf_op jit(solution)/shard_map/exchange/pallas_call | solution.py:265
  31.7 1.5 %finish.1 = (f32[524,1048]{1,0:T(8,128)}, f32[524,128]{1,0:T(8,128)}) custom-call(f32[524,1048]{1,0:T(8,128)S(1)} %get-tuple-element.5.gram_ref, bf16[528,2048]{1,0:T(8,128)(2,1)S(1)} %get-tuple-element.6.row_ref, bf16[2,64,16,128]{3,2,1,0:T(8,128)(2,1)S(1)} %get-tuple-element.7.moments_ref), custom_call_target="tpu_custom_call" | custom-call | tf_op jit(solution)/shard_map/finish/pallas_call | solution.py:300

commit v4 on v3

v4 whole, which is shorter than its diff:
```python
import jax
import jax.numpy as jnp
from jax import lax
from jax.experimental import pallas as pl
from jax.experimental.pallas import tpu as pltpu
from jax.sharding import PartitionSpec as P

MESH = pl.DeviceIdType.MESH
F32 = jnp.float32
BF16 = jnp.bfloat16
CHUNKS = (2048, 2048, 2048, 2048)
VMEM_KIB = 47000


def device_at(x, y, z, c):
    return ((y * 2 + lax.rem(z, 2)) * 2 + c, lax.div(z, 2) * 4 + x)


def one_hot(base, count):
    rank = 128
    k = lax.broadcasted_iota(jnp.int32, (count, rank), 0) + base
    t = lax.broadcasted_iota(jnp.int32, (count, rank), 1)
    start = rank + t * rank - lax.div(t * (t - 1), 2)
    quad_i = (k >= start) & (k < start + rank - t)
    offset = jnp.sum(jnp.where(quad_i, t - start, 0).astype(F32), axis=1, keepdims=True)
    linear = k < rank
    pick_i = jnp.where(quad_i | (linear & (t == k)), 1.0, 0.0).astype(BF16)
    pick_j = jnp.where(((t - k).astype(F32) == offset) & (k >= rank), 1.0, 0.0).astype(BF16)
    return pick_i, pick_j


def exchange_kernel(
    snap_hbm, rates_hbm, basis_hbm, gram_out, row_out, moments_out,
    states, moments, feat, acc, gram, snap, rates, basis, basis_t, part_s, part_m, land_s, land_m, pick_i, pick_j,
    load_sem, send_s, recv_s, send_m, recv_m,
    sg_send, sg_recv, mg_send, mg_recv, f_send, f_recv, out_sem, here,
):
    rows, reg = lax.axis_index("rows"), lax.axis_index("reg")
    c = lax.rem(rows, 2)
    zl = lax.rem(lax.div(rows, 2), 2)
    y = lax.div(rows, 4)
    x = lax.rem(reg, 4)
    zh = lax.div(reg, 4)
    z = zh * 2 + zl
    twin = device_at(x, y, z, 1 - c)

    def turn(v, d):
        return lax.rem(v + d, 4)

    group = [(dy, dz, dc) for dy in range(4) for dz in range(2) for dc in range(2)][1:]
    chips = sorted(
        ((dx, dy, dz) for dx in range(4) for dy in range(4) for dz in range(4)),
        key=lambda d: (sum(min(a, 4 - a) for a in d), d),
    )
    xs, ys, zs = ([turn(v, d) for d in range(4)] for v in (x, y, z))

    def group_row(dy, dz, dc):
        return (ys[dy] * 2 + lax.rem(zl + dz, 2)) * 2 + lax.rem(c + dc, 2)

    def chip(dx, dy, dz):
        return device_at(xs[dx], ys[dy], zs[dz], c)

    chunks = [pl.ds(sum(CHUNKS[:k]), depth) for k, depth in enumerate(CHUNKS)]
    loads = {}
    for i, k in [(i, k) for k in range(len(chunks)) for i in (0, 1)] + [(2, k) for k in range(len(chunks))]:
        at = chunks[k]
        src, dst = ((basis_hbm, basis), (snap_hbm, snap), (rates_hbm, rates))[i]
        loads[i, k] = pltpu.make_async_copy(src.at[at, :], dst.at[at, :], load_sem.at[i, k])
        loads[i, k].start()

    barrier = pltpu.get_barrier_semaphore()
    with jax.named_scope("signal"):
        for dy, dz, dc in group:
            pl.semaphore_signal(barrier, inc=1, device_id=(group_row(dy, dz, dc), reg), device_id_type=MESH)
        for dx in (1, 2, 3):
            pl.semaphore_signal(barrier, inc=1, device_id=chip(dx, 0, 0), device_id_type=MESH)
        across = chip(0, 0, 2)
        pl.semaphore_signal(barrier, inc=1, device_id=across, device_id_type=MESH)

    def all_of(ref, send, recv):
        return pltpu.make_async_remote_copy(
            src_ref=ref, dst_ref=ref, send_sem=send, recv_sem=recv, device_id=twin, device_id_type=MESH
        )

    def scatter(part, land, send, recv):
        for n, (dy, dz, dc) in sorted(enumerate(group), key=lambda p: -(min(p[1][0], 4 - p[1][0]) + p[1][1])):
            to = group_row(dy, dz, dc)
            pltpu.make_async_remote_copy(
                src_ref=part.at[to], dst_ref=land.at[n], send_sem=send, recv_sem=recv,
                device_id=(to, reg), device_id_type=MESH,
            ).start()

    def collect(part, land, send, recv):
        all_of(land, send, recv).wait_recv()
        piece = part[rows]
        for n in range(15):
            piece += land[n]
        return piece

    with jax.named_scope("proj_s"):
        total = jnp.zeros((128, 256), F32)
        for k, at in enumerate(chunks):
            loads[0, k].wait()
            loads[1, k].wait()
            turned = basis[at, :].T
            basis_t[:, at] = turned
            total += jnp.dot(turned, snap[at, :], preferred_element_type=F32)
        part_s[...] = total.T.reshape(16, 16, 128)
    with jax.named_scope("barrier_wait"):
        pl.semaphore_wait(barrier, 19)
    with jax.named_scope("send_s"):
        scatter(part_s, land_s, send_s, recv_s)
    for dx in (1, 2, 3):
        pl.semaphore_signal(here.at[0], inc=1, device_id=chip(dx, 0, 0), device_id_type=MESH)
    with jax.named_scope("proj_m"):
        total = jnp.zeros((128, 256), F32)
        for k, at in enumerate(chunks):
            loads[2, k].wait()
            total += jnp.dot(basis_t[:, at], rates[at, :], preferred_element_type=F32)
        part_m[...] = total.T.reshape(16, 16, 128)
    with jax.named_scope("here0"):
        pl.semaphore_wait(here.at[0], 3)
        pl.semaphore_signal(here.at[1], inc=1, device_id=across, device_id_type=MESH)
    with jax.named_scope("send_m"):
        scatter(part_m, land_m, send_m, recv_m)

    height, width = row_out.shape[2], acc.shape[1]
    bases = ((0, rows * 524, height), (height, reg * 1048, width), (height + width, (rows + 1 - 2 * c) * 524, height))
    with jax.named_scope("picks"):
        for at, base, count in bases:
            pick_i[at:at + count, :], pick_j[at:at + count, :] = one_hot(base, count)

    def far(a, b, v):
        return turn(v, (1 - c) * a + c * b)

    pairs = [(a, b) for a in range(4) for b in range(4)]
    far_x, far_y, far_z = ({p: far(*p, v) for p in pairs} for v in (x, y, z))

    def target(dx, dy, dz):
        return device_at(far_x[dx, dy], far_y[dy, dz], far_z[dz, dx], c)

    def gather(buf, send, recv):
        flat = buf.reshape(buf.shape[0] * buf.shape[1], *buf.shape[2:])

        def scatter_out(first, last):
            for n, d in list(enumerate(chips))[first:last]:
                pltpu.make_async_remote_copy(
                    src_ref=buf.at[c, 0], dst_ref=buf.at[c, n], send_sem=send, recv_sem=recv.at[n // 16 if n > 6 else 8],
                    device_id=target(*d), device_id_type=MESH,
                ).start()

        def arrive_near():
            all_of(buf.at[c, pl.ds(0, 6)], send, recv.at[8]).wait_recv()

        def arrive(n):
            all_of(buf.at[c, pl.ds(0, 9 if n == 0 else 16)], send, recv.at[n]).wait_recv()

        def pass_on(n):
            at = pl.ds(n * 16, 16)
            pltpu.make_async_remote_copy(
                src_ref=buf.at[c, at], dst_ref=buf.at[c, at], send_sem=send, recv_sem=recv.at[4 + n],
                device_id=twin, device_id_type=MESH,
            ).start()

        def from_twin(n):
            all_of(buf.at[1 - c, pl.ds(n * 16, 16)], send, recv.at[4 + n]).wait_recv()

        def drain(count):
            all_of(flat.at[pl.ds(0, count)], send, recv.at[0]).wait_send()

        return scatter_out, arrive_near, arrive, pass_on, from_twin, drain

    s_out, s_near, s_arrive, s_pass, s_twin, s_drain = gather(states, sg_send, sg_recv)
    m_out, m_near, m_arrive, m_pass, m_twin, m_drain = gather(moments, mg_send, mg_recv)

    def features(core, n, parts):
        s = states[core, n * 16:(n + 1) * 16].reshape(256, 128)
        hi = s.astype(BF16)
        lo = (s - hi.astype(F32)).astype(BF16)
        split = jnp.concatenate([hi, lo], axis=1)

        def select(pick, at, count):
            e = pick[at:at + count, :]
            return lax.dot_general(
                jnp.concatenate([e, e], axis=1), split, (((1,), (1,)), ((), ())), preferred_element_type=F32
            )

        for at, base, count in parts[::-1]:
            k = lax.broadcasted_iota(jnp.int32, (128, 256), 0) + base
            plus = jnp.where(k < 128, 1.0, 0.0)
            a, b = select(pick_i, at, count), select(pick_j, at, count)
            feat[core, n, at:at + 128, :] = (a[:128] * (b[:128] + plus)).astype(BF16)
            feat[core, n, at + 128:at + count, :] = (a[128:] * b[128:]).astype(BF16)
        for src, dst in ((pl.ds(height + width, height), pl.ds(0, height)), (pl.ds(height, width),) * 2)[:len(parts) // 3 * 2]:
            pltpu.make_async_remote_copy(
                src_ref=feat.at[c, n, src], dst_ref=feat.at[c, n, dst], send_sem=f_send, recv_sem=f_recv.at[n],
                device_id=twin, device_id_type=MESH,
            ).start()

    times = 8 * 256
    out_rows, out_cols = gram.shape
    shared = pl.ds(0, height + width)

    def accumulate(n):
        if n < 3:
            all_of(feat.at[1 - c, n, shared], f_send, f_recv.at[n]).wait_recv()
        for q in range(2):
            pltpu.make_async_copy(feat.at[q, n, pl.ds(0, height)], row_out.at[q, n], out_sem.at[0]).start()
        lhs = jnp.concatenate([feat[q, n, :height, :] for q in range(2)], axis=1)
        for at in range(0, width, 256):
            to = min(at + 256, width)
            rhs = jnp.concatenate([feat[q, n, height + at:height + to, :] for q in range(2)], axis=1)
            part = lax.dot_general(lhs, rhs, (((1,), (1,)), ((), ())), preferred_element_type=F32)
            if n:
                part += acc[:, at:to]
            if n < 3:
                acc[:, at:to] = part
            else:
                to = min(to, out_cols)
                gram[:, at:to] = part[:out_rows, :to - at] * (1.0 / times)

    outs = [(moments, moments_out, 2), (gram, gram_out, 1)]

    with jax.named_scope("rs_s"):
        states[c, 0] = collect(part_s, land_s, send_s, recv_s)
    with jax.named_scope("here1"):
        pl.semaphore_wait(here.at[1], 1)
    with jax.named_scope("s_out"):
        s_out(1, 32)

        @pl.when(c == 0)
        def _():
            s_out(32, 64)

    with jax.named_scope("near"):
        s_near()

    @pl.when(c == 1)
    def _():
        s_out(32, 64)

    for n in range(4):
        with jax.named_scope(f"a{n}"):
            s_arrive(n)
            if n == 3:
                s_pass(n)
        if n == 1:
            with jax.named_scope("m_out"):
                moments[c, 0] = collect(part_m, land_m, send_m, recv_m).astype(BF16)
                m_out(1, 64)
        with jax.named_scope(f"f{n}"):
            features(c, n, bases if n < 3 else bases[:2])
        if n:
            with jax.named_scope(f"g{n - 1}"):
                accumulate(n - 1)
    with jax.named_scope("t3"):
        s_twin(3)
    with jax.named_scope("ft3"):
        features(1 - c, 3, bases[:2])
    with jax.named_scope("m_arrive"):
        m_near()
        for n in range(4):
            m_arrive(n)
            m_pass(n)
    with jax.named_scope("g3"):
        accumulate(3)
    pltpu.make_async_copy(gram, gram_out, out_sem.at[1]).start()
    with jax.named_scope("m_twin"):
        for k in range(4):
            m_twin(k)
    pltpu.make_async_copy(moments, moments_out, out_sem.at[2]).start()
    with jax.named_scope("drain"):
        all_of(land_s, send_s, recv_s).wait_send()
        all_of(land_m, send_m, recv_m).wait_send()
        s_drain(79)
        m_drain(127)
        all_of(feat.at[c, pl.ds(0, 3), shared], f_send, f_recv.at[0]).wait_send()
        for src, dst, n in [(row_out, row_out, 0)] + outs:
            pltpu.make_async_copy(src, dst, out_sem.at[n]).wait()


def finish_kernel(gram_ref, row_ref, moments_ref, gram_out, rhs_out, rhs_ref, sem):
    copy = pltpu.make_async_copy(gram_ref, gram_out, sem.at[0])
    copy.start()
    blocks = [(q, n) for q in range(2) for n in range(4)]
    with jax.named_scope("rhs"):
        rhs = jnp.dot(
            jnp.concatenate([row_ref[q, n] for q, n in blocks], axis=1),
            jnp.concatenate([moments_ref[q, n * 16:(n + 1) * 16].reshape(256, 128) for q, n in blocks], axis=0),
            preferred_element_type=F32,
        )
        rhs_ref[...] = rhs[:rhs_ref.shape[0]] * (1.0 / (256 * len(blocks)))
    with jax.named_scope("k2wait"):
        rhs_copy = pltpu.make_async_copy(rhs_ref, rhs_out, sem.at[1])
        rhs_copy.start()
        copy.wait()
        rhs_copy.wait()


def per_device(snapshots, rates, basis):
    n, t = snapshots.shape
    rank = basis.shape[1]
    width = rank + rank * (rank + 1) // 2
    assert rank == 128 and t == 256 and n == sum(CHUNKS)
    assert lax.axis_size("rows") == 16 and lax.axis_size("reg") == 8
    row_width, col_width = width // 16, width // 8
    row_pad, col_pad = pl.cdiv(row_width, 16) * 16, pl.cdiv(col_width, 16) * 16
    dma = pltpu.SemaphoreType.DMA
    gram, row_feat, moments = pl.pallas_call(
        exchange_kernel,
        out_shape=(
            jax.ShapeDtypeStruct((row_width, col_width), F32),
            jax.ShapeDtypeStruct((2, 4, row_pad, t), BF16),
            jax.ShapeDtypeStruct((2, 64, 16, rank), BF16),
        ),
        in_specs=[pl.BlockSpec(memory_space=pl.ANY)] * 3,
        out_specs=[pl.BlockSpec(memory_space=pl.ANY)] * 3,
        scratch_shapes=[
            pltpu.VMEM((2, 64, 16, rank), F32),
            pltpu.VMEM((2, 64, 16, rank), BF16),
            pltpu.VMEM((2, 4, 2 * row_pad + col_pad, t), BF16),
            pltpu.VMEM((row_pad, col_pad), F32),
            pltpu.VMEM((row_width, col_width), F32),
            pltpu.VMEM((n, t), BF16),
            pltpu.VMEM((n, t), BF16),
            pltpu.VMEM((n, rank), BF16),
            pltpu.VMEM((rank, n), BF16),
            pltpu.VMEM((16, 16, rank), F32),
            pltpu.VMEM((16, 16, rank), F32),
            pltpu.VMEM((15, 16, rank), F32),
            pltpu.VMEM((15, 16, rank), F32),
            pltpu.VMEM((2 * row_pad + col_pad, rank), BF16),
            pltpu.VMEM((2 * row_pad + col_pad, rank), BF16),
            dma((3, len(CHUNKS))),
            dma, dma, dma, dma,
            dma, dma((9,)), dma, dma((9,)), dma, dma((3,)), dma((3,)), pltpu.SemaphoreType.REGULAR((2,)),
        ],
        compiler_params=pltpu.CompilerParams(
            collective_id=0, has_side_effects=True, vmem_limit_bytes=VMEM_KIB << 10
        ),
        name="exchange",
    )(*[pltpu.with_memory_space_constraint(a, pltpu.MemorySpace.HBM) for a in (snapshots, rates, basis)])
    return pl.pallas_call(
        finish_kernel,
        out_shape=(
            jax.ShapeDtypeStruct((row_width, col_width), F32),
            jax.ShapeDtypeStruct((row_width, rank), F32),
        ),
        in_specs=[
            pl.BlockSpec(memory_space=pl.ANY),
            pl.BlockSpec(memory_space=pltpu.VMEM),
            pl.BlockSpec(memory_space=pltpu.VMEM),
        ],
        out_specs=[pl.BlockSpec(memory_space=pl.ANY)] * 2,
        scratch_shapes=[pltpu.VMEM((row_width, rank), F32), dma((2,))],
        compiler_params=pltpu.CompilerParams(vmem_limit_bytes=16 << 20),
        name="finish",
    )(gram, row_feat, moments)


def solution(mesh):
    return jax.shard_map(
        per_device,
        mesh=mesh,
        in_specs=(P("rows", "reg"), P("rows", "reg"), P("rows", None)),
        out_specs=(P("rows", "reg"), P("rows", None)),
        check_vma=False,
    )
```

time: 33.4 us -> 31.4 us (0.940)
  Pallas kernels: 32.6 us -> 30.7 us
    pallas_call x1, Pallas kernels: 31.1 us -> 29.1 us  [per_device(): pl.pallas_call(exchange_kernel, out_shape=(jax.ShapeDtypeStruct((row_widt...]
where the time goes in v4:
time: 31.4 us; the launch traced here: 31.3 us
  Pallas kernels  30.7 us (98%)
  between operations  0.64 us (2%)
    pallas_call x1, Pallas kernels, per_device(): pl.pallas_call(exchange_kernel, out_shape=(jax.ShapeDtypeStruct((row_widt...  29.1 us
    pallas_call x1, Pallas kernels, per_device(): pl.pallas_call(finish_kernel, out_shape=(jax.ShapeDtypeStruct((row_width,...  1.53 us

profile of v4, /device:TPU:1, one launch (start us, length us, event | category | flops | bytes accessed | tf_op | source)
XLA Modules:
  0.0 31.3 jit_solution(8258394841063476718)
XLA Ops:
  0.6 29.1 %exchange.1 = (f32[524,1048]{1,0:T(8,128)S(1)}, bf16[2,4,528,256]{3,2,1,0:T(8,128)(2,1)S(1)}, bf16[2,64,16,128]{3,2,1,0:T(8,128)(2,1)S(1)}) custom-call(bf16[8192,256]{1,0:T(8,128)(2,1)} %snap_hbm.1, bf16[8192,256]{1,0:T(8,128)(2,1)} %rates_hbm.1, bf16[8192,128]{1,0:T(8,128)(2,1)} %basis_hbm.1), custom_call_target="tpu_custom_call" | custom-call | tf_op jit(solution)/shard_map/exchange/pallas_call | solution.py:309
  29.8 1.5 %finish.1 = (f32[524,1048]{1,0:T(8,128)}, f32[524,128]{1,0:T(8,128)}) custom-call(f32[524,1048]{1,0:T(8,128)S(1)} %get-tuple-element.5.gram_ref, bf16[2,4,528,256]{3,2,1,0:T(8,128)(2,1)S(1)} %get-tuple-element.6.row_ref, bf16[2,64,16,128]{3,2,1,0:T(8,128)(2,1)S(1)} %get-tuple-element.7.moments_ref), custom_call_target="tpu_custom_call" | custom-call | tf_op jit(solution)/shard_map/finish/pallas_call | solution.py:343

commit v5 on v4

--- a/solution.py
+++ b/solution.py
@@ -31,8 +31,8 @@
 
 def exchange_kernel(
     snap_hbm, rates_hbm, basis_hbm, gram_out, row_out, moments_out,
-    states, moments, feat, acc, gram, snap, rates, basis, basis_t, part_s, part_m, land_s, land_m, pick_i, pick_j,
-    load_sem, send_s, recv_s, send_m, recv_m,
+    states, moments, feat, acc, gram, snap, rates, basis, basis_t, part_s, part_m, half_m, land_s, land_m, land_h, pick_i, pick_j,
+    load_sem, send_s, recv_s, send_m, recv_m, send_h, recv_h,
     sg_send, sg_recv, mg_send, mg_recv, f_send, f_recv, out_sem, here,
 ):
     rows, reg = lax.axis_index("rows"), lax.axis_index("reg")
@@ -90,10 +90,12 @@
                 device_id=(to, reg), device_id_type=MESH,
             ).start()
 
-    def collect(part, land, send, recv):
+    pair = [d for d in group if not d[2]]
+
+    def collect(part, at, land, send, recv):
         all_of(land, send, recv).wait_recv()
-        piece = part[rows]
-        for n in range(15):
+        piece = part[at]
+        for n in range(land.shape[0]):
             piece += land[n]
         return piece
 
@@ -117,12 +119,15 @@
         for k, at in enumerate(chunks):
             loads[2, k].wait()
             total += jnp.dot(basis_t[:, at], rates[at, :], preferred_element_type=F32)
-        part_m[...] = total.T.reshape(16, 16, 128)
+        part_m[...] = total.T.reshape(8, 2, 16, 128)
     with jax.named_scope("here0"):
         pl.semaphore_wait(here.at[0], 3)
         pl.semaphore_signal(here.at[1], inc=1, device_id=across, device_id_type=MESH)
     with jax.named_scope("send_m"):
-        scatter(part_m, land_m, send_m, recv_m)
+        pltpu.make_async_remote_copy(
+            src_ref=part_m.at[:, 1 - c], dst_ref=land_h, send_sem=send_h, recv_sem=recv_h,
+            device_id=twin, device_id_type=MESH,
+        ).start()
 
     height, width = row_out.shape[2], acc.shape[1]
     bases = ((0, rows * 524, height), (height, reg * 1048, width), (height + width, (rows + 1 - 2 * c) * 524, height))
@@ -221,8 +226,17 @@
 
     outs = [(moments, moments_out, 2), (gram, gram_out, 1)]
 
+    with jax.named_scope("half_m"):
+        all_of(land_h, send_h, recv_h).wait_recv()
+        half_m[...] = part_m[:, c] + land_h[...]
+        for n, (dy, dz, _) in enumerate(pair):
+            to = ys[dy] * 2 + lax.rem(zl + dz, 2)
+            pltpu.make_async_remote_copy(
+                src_ref=half_m.at[to], dst_ref=land_m.at[n], send_sem=send_m, recv_sem=recv_m,
+                device_id=(to * 2 + c, reg), device_id_type=MESH,
+            ).start()
     with jax.named_scope("rs_s"):
-        states[c, 0] = collect(part_s, land_s, send_s, recv_s)
+        states[c, 0] = collect(part_s, rows, land_s, send_s, recv_s)
     with jax.named_scope("here1"):
         pl.semaphore_wait(here.at[1], 1)
     with jax.named_scope("s_out"):
@@ -240,14 +254,14 @@
         s_out(32, 64)
 
     for n in range(4):
+        if n == 1:
+            with jax.named_scope("m_out"):
+                moments[c, 0] = collect(half_m, lax.div(rows, 2), land_m, send_m, recv_m).astype(BF16)
+                m_out(1, 64)
         with jax.named_scope(f"a{n}"):
             s_arrive(n)
             if n == 3:
                 s_pass(n)
-        if n == 1:
-            with jax.named_scope("m_out"):
-                moments[c, 0] = collect(part_m, land_m, send_m, recv_m).astype(BF16)
-                m_out(1, 64)
         with jax.named_scope(f"f{n}"):
             features(c, n, bases if n < 3 else bases[:2])
         if n:
@@ -272,6 +286,7 @@
     with jax.named_scope("drain"):
         all_of(land_s, send_s, recv_s).wait_send()
         all_of(land_m, send_m, recv_m).wait_send()
+        all_of(land_h, send_h, recv_h).wait_send()
         s_drain(79)
         m_drain(127)
         all_of(feat.at[c, pl.ds(0, 3), shared], f_send, f_recv.at[0]).wait_send()
@@ -326,13 +341,15 @@
             pltpu.VMEM((n, rank), BF16),
             pltpu.VMEM((rank, n), BF16),
             pltpu.VMEM((16, 16, rank), F32),
-            pltpu.VMEM((16, 16, rank), F32),
+            pltpu.VMEM((8, 2, 16, rank), F32),
+            pltpu.VMEM((8, 16, rank), F32),
             pltpu.VMEM((15, 16, rank), F32),
-            pltpu.VMEM((15, 16, rank), F32),
+            pltpu.VMEM((7, 16, rank), F32),
+            pltpu.VMEM((8, 16, rank), F32),
             pltpu.VMEM((2 * row_pad + col_pad, rank), BF16),
             pltpu.VMEM((2 * row_pad + col_pad, rank), BF16),
             dma((3, len(CHUNKS))),
-            dma, dma, dma, dma,
+            dma, dma, dma, dma, dma, dma,
             dma, dma((9,)), dma, dma((9,)), dma, dma((3,)), dma((3,)), pltpu.SemaphoreType.REGULAR((2,)),
         ],
         compiler_params=pltpu.CompilerParams(

time: 31.4 us -> 31.2 us (level)
  no operation moved by 1% of the time
where the time goes in v5:
time: 31.2 us; the launch traced here: 31.1 us
  Pallas kernels  30.5 us (98%)
  between operations  0.64 us (2%)
    pallas_call x1, Pallas kernels, per_device(): pl.pallas_call(exchange_kernel, out_shape=(jax.ShapeDtypeStruct((row_widt...  28.9 us
    pallas_call x1, Pallas kernels, per_device(): pl.pallas_call(finish_kernel, out_shape=(jax.ShapeDtypeStruct((row_width,...  1.53 us

profile of v5, /device:TPU:1, one launch (start us, length us, event | category | flops | bytes accessed | tf_op | source)
XLA Modules:
  0.0 31.1 jit_solution(9006188542123728639)
XLA Ops:
  0.6 28.9 %exchange.1 = (f32[524,1048]{1,0:T(8,128)S(1)}, bf16[2,4,528,256]{3,2,1,0:T(8,128)(2,1)S(1)}, bf16[2,64,16,128]{3,2,1,0:T(8,128)(2,1)S(1)}) custom-call(bf16[8192,256]{1,0:T(8,128)(2,1)} %snap_hbm.1, bf16[8192,256]{1,0:T(8,128)(2,1)} %rates_hbm.1, bf16[8192,128]{1,0:T(8,128)(2,1)} %basis_hbm.1), custom_call_target="tpu_custom_call" | custom-call | tf_op jit(solution)/shard_map/exchange/pallas_call | solution.py:324
  29.6 1.5 %finish.1 = (f32[524,1048]{1,0:T(8,128)}, f32[524,128]{1,0:T(8,128)}) custom-call(f32[524,1048]{1,0:T(8,128)S(1)} %get-tuple-element.5.gram_ref, bf16[2,4,528,256]{3,2,1,0:T(8,128)(2,1)S(1)} %get-tuple-element.6.row_ref, bf16[2,64,16,128]{3,2,1,0:T(8,128)(2,1)S(1)} %get-tuple-element.7.moments_ref), custom_call_target="tpu_custom_call" | custom-call | tf_op jit(solution)/shard_map/finish/pallas_call | solution.py:360

commit v6 on v5

--- a/solution.py
+++ b/solution.py
@@ -251,7 +251,8 @@
 
     @pl.when(c == 1)
     def _():
-        s_out(32, 64)
+        s_out(32, 48)
+
 
     for n in range(4):
         if n == 1:
@@ -260,6 +261,8 @@
                 m_out(1, 64)
         with jax.named_scope(f"a{n}"):
             s_arrive(n)
+            if n == 0:
+                pl.when(c == 1)(lambda: s_out(48, 64))
             if n == 3:
                 s_pass(n)
         with jax.named_scope(f"f{n}"):

time: 31.2 us -> 31.2 us (level)
  no operation moved by 1% of the time
where the time goes in v6:
time: 31.2 us; the launch traced here: 31.1 us
  Pallas kernels  30.5 us (98%)
  between operations  0.64 us (2%)
    pallas_call x1, Pallas kernels, per_device(): pl.pallas_call(exchange_kernel, out_shape=(jax.ShapeDtypeStruct((row_widt...  28.9 us
    pallas_call x1, Pallas kernels, per_device(): pl.pallas_call(finish_kernel, out_shape=(jax.ShapeDtypeStruct((row_width,...  1.53 us

profile of v6, /device:TPU:1, one launch (start us, length us, event | category | flops | bytes accessed | tf_op | source)
XLA Modules:
  0.0 31.1 jit_solution(9273600451528936338)
XLA Ops:
  0.6 28.9 %exchange.1 = (f32[524,1048]{1,0:T(8,128)S(1)}, bf16[2,4,528,256]{3,2,1,0:T(8,128)(2,1)S(1)}, bf16[2,64,16,128]{3,2,1,0:T(8,128)(2,1)S(1)}) custom-call(bf16[8192,256]{1,0:T(8,128)(2,1)} %snap_hbm.1, bf16[8192,256]{1,0:T(8,128)(2,1)} %rates_hbm.1, bf16[8192,128]{1,0:T(8,128)(2,1)} %basis_hbm.1), custom_call_target="tpu_custom_call" | custom-call | tf_op jit(solution)/shard_map/exchange/pallas_call | solution.py:327
  29.6 1.5 %finish.1 = (f32[524,1048]{1,0:T(8,128)}, f32[524,128]{1,0:T(8,128)}) custom-call(f32[524,1048]{1,0:T(8,128)S(1)} %get-tuple-element.5.gram_ref, bf16[2,4,528,256]{3,2,1,0:T(8,128)(2,1)S(1)} %get-tuple-element.6.row_ref, bf16[2,64,16,128]{3,2,1,0:T(8,128)(2,1)S(1)} %get-tuple-element.7.moments_ref), custom_call_target="tpu_custom_call" | custom-call | tf_op jit(solution)/shard_map/finish/pallas_call | solution.py:363
